TPU v7x, 32 devices: a whole 2x2x4 slice. The times are simulated.
32 devices in a mesh: tm: 4 (over y, core), chan: 8 (over z, x).
Axes of the slice: x: 2, y: 2, z: 4, core: 2. Of those that a mesh axis runs over, the one named last changes fastest.
Arguments:
- recordings: float32 [4, 256, 8, 512], P('tm', None, 'chan')
- gap_start: int32 [4, 256, 8], P('tm', None, 'chan'), may hold values from 0 to 511
- dropout_extent: int32 [4, 256, 8], P('tm', None, 'chan'), may hold values from 0 to 256
- filter_taps: float32 [128], replicated, may hold values from -0.5 to 0.5
- source_channel: int32 [32], P('chan'), may hold values from 0 to 255
- receiver_block: int32 [32], P('chan'), may hold values from 0 to 3
Outputs:
- stacks: float32 [128, 32, 1024], P('tm', 'chan')
All inputs are finite; a program needn't handle non-finite values.
Results may differ from a plain program's by a relative error of at most 0.0031.
Values may be sent and summed in bfloat16 or wider, within the bound.
No kernel may reach another device: no remote copies, remote signals or barrier semaphores. Data moves between devices by JAX's collectives and lax.ppermute only.
A program may use at most 64 MiB of HBM per device.

v0:
```python
import math
import jax
import jax.numpy as jnp
import numpy as np
from jax import lax
from jax.sharding import PartitionSpec as P

BLOCK = 128
MAX_LAG = 512


def passed_along(block, axis, distance):
    devices = range(lax.axis_size(axis))
    route = [(i - distance, i) for i in devices if i - distance in devices]
    return lax.ppermute(block, axis, route)


def valid_mask(starts, lengths, sample_count):
    position = jnp.arange(sample_count, dtype=jnp.int32)
    inside = (position >= starts[..., None]) & (position < starts[..., None] + lengths[..., None])
    return jnp.where(inside, 0.0, 1.0).astype(jnp.float32)


def fir_filter(signal, filter_taps):
    tap_count = filter_taps.shape[0]
    channel_count, sample_count = signal.shape
    pieces = signal.reshape(channel_count, sample_count // tap_count, tap_count)
    earlier = jnp.concatenate([jnp.zeros_like(pieces[:, :1]), pieces[:, :-1]], axis=1)
    position = jnp.arange(tap_count, dtype=jnp.int32)
    offset = position[None, :] - position[:, None]
    present_filter_tap = jnp.where(
        offset >= 0, filter_taps[jnp.clip(offset, 0, tap_count - 1)], 0.0
    )
    carried_tap = jnp.where(
        offset < 0, filter_taps[jnp.clip(offset + tap_count, 0, tap_count - 1)], 0.0
    )
    result = jnp.einsum("cki,im->ckm", pieces, present_filter_tap, precision=lax.Precision.HIGHEST)
    result = result + jnp.einsum(
        "cki,im->ckm", earlier, carried_tap, precision=lax.Precision.HIGHEST
    )
    return result.reshape(channel_count, sample_count)


def normalize_traces(filtered, retained_mask):
    counted = jnp.sum(retained_mask, axis=-1, keepdims=True)
    mean_square = jnp.sum(filtered * filtered * retained_mask, axis=-1, keepdims=True) / counted
    return (filtered * retained_mask * lax.rsqrt(mean_square + 1e-05)).astype(jnp.bfloat16)


def correlate_batch(sources, receivers, max_lag):
    sample_count = sources.shape[-1]
    tile_width = math.gcd(math.gcd(max_lag, sample_count), 128)
    tile_count = sample_count // tile_width + 1
    edge = jnp.zeros((sources.shape[0], tile_width), sources.dtype)
    source_padded = jnp.concatenate([edge, sources, edge], axis=1)
    row_table = (
        np.arange(tile_count * tile_width)[:, None] - np.arange(tile_width)[None, :] + tile_width
    )
    lag_tiles = source_padded[:, row_table]
    lag_pad = jnp.zeros((receivers.shape[0], receivers.shape[1], max_lag), receivers.dtype)
    receivers_padded = jnp.concatenate([lag_pad, receivers, lag_pad], axis=2)
    columns = []
    for lag_block in range(2 * max_lag // tile_width):
        segment_taper = receivers_padded[
            :, :, lag_block * tile_width : lag_block * tile_width + tile_count * tile_width
        ]
        columns.append(
            jnp.einsum("scz,szu->csu", segment_taper, lag_tiles, preferred_element_type=jnp.float32)
        )
    return jnp.concatenate(columns, axis=2)


def select_blocks(blocks, receiver_block, pair_count):
    picked = [
        lax.dynamic_slice_in_dim(blocks, receiver_block[pair_index], 1, axis=0)
        for pair_index in range(pair_count)
    ]
    return jnp.concatenate(picked, axis=0)


def neighbour_blocks(owned_rows):
    return passed_along(owned_rows, "chan", -1)


def local(recordings, gap_start, dropout_extent, filter_taps, source_channel, receiver_block):
    traces = recordings[0, :, 0, :]
    retained_mask = valid_mask(gap_start[0, :, 0], dropout_extent[0, :, 0], traces.shape[1])
    filtered = fir_filter(traces * retained_mask, filter_taps)
    normalized = normalize_traces(filtered, retained_mask)
    round_count, sample_count = normalized.shape
    regrouped = lax.all_to_all(
        normalized.reshape(round_count, 1, sample_count),
        "chan",
        split_axis=0,
        concat_axis=1,
        tiled=True,
    )
    owned_rows = regrouped.reshape(round_count, sample_count)
    sources = owned_rows[source_channel]
    segment_count = lax.axis_size("tm")
    factor = 1.0 / math.sqrt(sample_count * segment_count)
    pair_count = sources.shape[0]
    block_count = round_count // BLOCK
    following = neighbour_blocks(owned_rows)
    blocks = jnp.concatenate([owned_rows, following], axis=0).reshape(
        2 * block_count, BLOCK, sample_count
    )
    receivers = select_blocks(blocks, receiver_block, pair_count)
    stack_terms = correlate_batch(sources, receivers, MAX_LAG) * factor
    stacks = lax.psum_scatter(stack_terms, "tm", scatter_dimension=0, tiled=True)
    return stacks


def solution(mesh):
    return jax.shard_map(
        local,
        mesh=mesh,
        in_specs=(
            P("tm", None, "chan", None),
            P("tm", None, "chan"),
            P("tm", None, "chan"),
            P(),
            P("chan"),
            P("chan"),
        ),
        out_specs=P("tm", "chan", None),
        check_vma=False,
    )
```

profile of v0, /device:TPU:0, one launch (start us, length us, event | category | flops | bytes accessed | tf_op | source)
XLA Modules:
  0.0 605.1 jit_solution(15314912430270999718)
XLA Ops:
  6.5 0.0 copy-start
  6.6 1.2 copy.46
  7.9 0.0 copy-done
  7.9 97.2 %gather_fusion = f32[16384]{0:T(1024)S(1)} fusion(f32[128]{0:T(128)S(1)} %copy-done, s32[16384]{0:T(1024)S(1)} %fusion.21), kind=kCustom, calls=%fused_computation | custom fusion | bytes 196608 | tf_op jit(solution)/shard_map/gather | solution.py:32
  105.1 0.0 copy-start.2
  105.1 0.0 copy-start.4
  105.1 97.2 %gather_fusion.1 = f32[16384]{0:T(1024)S(1)} fusion(f32[128]{0:T(128)S(1)} %copy-done, s32[16384]{0:T(1024)S(1)} %fusion.23), kind=kCustom, calls=%fused_computation.1 | custom fusion | bytes 196608 | tf_op jit(solution)/shard_map/gather | solution.py:35
  202.3 0.0 copy-done.2
  202.3 0.0 copy-done.4
  202.4 0.2 select_reduce_fusion
  202.6 0.2 select_multiply_fusion.1
  202.8 0.6 fusion.25
  203.4 0.0 copy-start.1
  203.4 0.7 fusion.16
  204.2 0.2 copy.63
  204.4 0.2 multiply_convert_fusion
  204.6 0.5 broadcast.235
  205.1 0.8 reduce.1
  205.9 0.9 reshape.270
  206.8 7.2 %all-to-all-start = ((bf16[8,2,8192]{2,1,0:T(2,128)(2,1)}), bf16[8,2,8192]{2,1,0:T(2,128)(2,1)S(1)}, u32[]{:S(2)}, u32[]{:S(2)}) async-start(bf16[8,2,8192]{2,1,0:T(2,128)(2,1)} %reshape.270), calls=%async_computation | async-start | bytes 524288 | tf_op jit(solution)/shard_map/all_to_all | solution.py:91
  214.0 0.0 all-reduce.6.cloned.1.call-start
  214.2 8.8 %all-to-all-done = bf16[8,2,8192]{2,1,0:T(2,128)(2,1)S(1)} async-done(((bf16[8,2,8192]{2,1,0:T(2,128)(2,1)}), bf16[8,2,8192]{2,1,0:T(2,128)(2,1)S(1)}, u32[]{:S(2)}, u32[]{:S(2)}) %all-to-all-start) | async-done | bytes 262176 | tf_op jit(solution)/shard_map/all_to_all | solution.py:91
  223.0 0.3 reshape.271
  223.3 0.2 copy.66
  223.4 1.3 collective-permute-start
  224.7 0.0 copy-done.3
  224.8 0.7 fusion.47
  233.0 0.6 gather_fusion.2
  233.6 0.2 copy.54
  233.8 286.2 %gather_fusion.3 = bf16[81920,4]{1,0:T(8,128)(2,1)} fusion(bf16[4,768]{0,1:T(8,128)(2,1)S(1)} %copy.54, s32[81920]{0:T(1024)S(1)} %broadcast_clamp_fusion), kind=kCustom, calls=%fused_computation.3 | custom fusion | bytes 1638400 | tf_op jit(solution)/shard_map/gather | solution.py:59
  520.0 19.5 %copy.55 = bf16[640,128,4]{0,1,2:T(8,128)(2,1)S(1)} copy(bf16[640,128,4]{2,1,0:T(8,128)(2,1)} %bitcast.95) | data formatting | bytes 1310720 | tf_op jit(solution)/shard_map/gather | solution.py:59
  539.5 0.0 collective-permute-done
  539.6 0.1 pad_maximum_fusion.1
  539.6 0.3 fusion.7
  540.0 0.3 fusion.6
  540.3 0.3 fusion.5
  540.6 0.4 fusion.4
  541.0 0.4 fusion.3
  541.4 0.3 fusion.2
  541.7 0.3 fusion.1
  542.1 0.3 fusion
  542.4 0.2 broadcast_multiply_fusion
  542.6 2.0 copy.56
  544.6 0.0 all-reduce.6.cloned.1.call-update
  544.7 0.6 copy-done.6
  545.3 0.6 dynamic-slice
  546.5 49.9 %all-reduce.6.cloned.1.call-done = f32[128,4,1024]{2,1,0:T(4,128)} async-done(((f32[128,4,1024]{2,1,0:T(4,128)}), f32[128,4,1024]{2,1,0:T(4,128)}) %all-reduce.6.cloned.1.call-update) | async-done | bytes 2097168
  596.4 1.9 constant_dynamic-slice_fusion.4
  (18 shorter events, 0.3 us)
Async XLA Ops:
  6.5 1.3 copy-start
  105.1 97.2 %copy-start.2 = (s32[1,256,1]{1,2,0:T(1,128)S(1)}, s32[1,256,1]{1,2,0:T(1,128)}, u32[]{:S(2)}) copy-start(s32[1,256,1]{1,2,0:T(1,128)} %param.9) | copy-start | bytes 3076
  105.1 97.2 %copy-start.4 = (s32[1,256,1]{1,2,0:T(1,128)S(1)}, s32[1,256,1]{1,2,0:T(1,128)}, u32[]{:S(2)}) copy-start(s32[1,256,1]{1,2,0:T(1,128)} %param.10) | copy-start | bytes 3076
  203.4 10.7 %copy-start.1 = (s32[81920]{0:T(1024)S(1)}, s32[81920]{0:T(1024)}, u32[]{:S(2)}) copy-start(s32[81920]{0:T(1024)} %constant.48) | copy-start | bytes 983044
  204.2 10.0 %copy-start.5 = (s32[4]{0:T(128)S(1)}, s32[4]{0:T(128)}, u32[]{:S(2)}) copy-start(s32[4]{0:T(128)} %param.12) | copy-start | bytes 52
  205.1 19.6 %copy-start.3 = (s32[4]{0:T(128)S(1)}, s32[4]{0:T(128)}, u32[]{:S(2)}) copy-start(s32[4]{0:T(128)} %param.13) | copy-start | bytes 52
  206.8 16.2 %all-to-all-start = ((bf16[8,2,8192]{2,1,0:T(2,128)(2,1)}), bf16[8,2,8192]{2,1,0:T(2,128)(2,1)S(1)}, u32[]{:S(2)}, u32[]{:S(2)}) async-start(bf16[8,2,8192]{2,1,0:T(2,128)(2,1)} %reshape.270), calls=%async_computation | async-start | bytes 524288 | tf_op jit(solution)/shard_map/all_to_all | solution.py:91
  214.0 382.4 %all-reduce.6.cloned.1.call-start = ((), (), s32[]{:S(2)}) async-start(), calls=%async_computation.1 | async-start | bytes 4194304
  223.4 316.0 %collective-permute-start = (bf16[256,512]{1,0:T(8,128)(2,1)S(1)}, bf16[256,512]{1,0:T(8,128)(2,1)S(1)}, u32[]{:S(2)}, u32[]{:S(2)}) collective-permute-start(bf16[256,512]{1,0:T(8,128)(2,1)S(1)} %bitcast.99), channel_id=1, source_target_pairs={{1,0},{2,1},{3,2},{4,3},{5,4},{6,5},{7,6},{9,8},{10,9},{11,10},{12... | collective-permute-start | bytes 786440 | tf_op jit(solution)/shard_map/ppermute | solution.py:15
  544.6 0.7 copy-start.6
Sparse Core Ops, SparseCore 0:
  544.8 51.5 all-reduce.5
where the time goes:
time: 606 us; the launch traced here: 605 us
  local copies, waits for them, and re-layouts  510 us (84%)
  waiting for transfers between devices  58.7 us (10%)
  between operations  21.9 us (4%)
  starting transfers between devices  8.58 us (1%)
    gather x2, local copies, waits for them, and re-layouts, correlate_batch(): lag_tiles = source_padded[:, row_table]  306 us
    gather x1, local copies, waits for them, and re-layouts, fir_filter(): filter_taps[jnp.clip(offset, 0, tap_count - 1)]  97.2 us
    gather x1, local copies, waits for them, and re-layouts, fir_filter(): filter_taps[jnp.clip(offset + tap_count, 0, tap_count - 1)]  97.2 us
    unnamed x2, waiting for transfers between devices  49.9 us
  transfers between devices with their start and end apart: 3, of which 2 were waited for; matrix products, arithmetic and copies ran while one was open for 51% of the time, Pallas kernels for 0%

commit v1 on v0

--- a/solution.py
+++ b/solution.py
@@ -88,12 +88,18 @@
     filtered = fir_filter(traces * retained_mask, filter_taps)
     normalized = normalize_traces(filtered, retained_mask)
     round_count, sample_count = normalized.shape
-    regrouped = lax.all_to_all(
-        normalized.reshape(round_count, 1, sample_count),
-        "chan",
-        split_axis=0,
-        concat_axis=1,
-        tiled=True,
+    regrouped = jnp.concatenate(
+        lax.all_to_all(
+            jnp.stack(
+                jnp.split(
+                    normalized.reshape(round_count, 1, sample_count), lax.axis_size("chan"), axis=0
+                )
+            ),
+            "chan",
+            0,
+            0,
+        ),
+        axis=1,
     )
     owned_rows = regrouped.reshape(round_count, sample_count)
     sources = owned_rows[source_channel]

time: 606 us -> 606 us (level)
  transfers between devices with their start and end apart: 3 -> 3, of which waited for: 2 -> 2; matrix products, arithmetic and copies ran while one was open for 51% -> 50% of each run, Pallas kernels for 0% -> 0%
where the time goes in v1:
time: 606 us; the launch traced here: 605 us
  local copies, waits for them, and re-layouts  511 us (84%)
  waiting for transfers between devices  58.7 us (10%)
  between operations  21.9 us (4%)
  starting transfers between devices  8.58 us (1%)
    gather x2, local copies, waits for them, and re-layouts, correlate_batch(): lag_tiles = source_padded[:, row_table]  304 us
    gather x1, local copies, waits for them, and re-layouts, fir_filter(): filter_taps[jnp.clip(offset, 0, tap_count - 1)]  97.2 us
    gather x1, local copies, waits for them, and re-layouts, fir_filter(): filter_taps[jnp.clip(offset + tap_count, 0, tap_count - 1)]  97.2 us
    unnamed x2, waiting for transfers between devices  49.9 us
  transfers between devices with their start and end apart: 3, of which 2 were waited for; matrix products, arithmetic and copies ran while one was open for 50% of the time, Pallas kernels for 0%

profile of v1, /device:TPU:0, one launch (start us, length us, event | category | flops | bytes accessed | tf_op | source)
XLA Modules:
  0.0 605.5 jit_solution(2864777512462318946)
XLA Ops:
  6.6 1.2 copy.25
  7.9 97.2 %gather_fusion = f32[16384]{0:T(1024)S(1)} fusion(f32[128]{0:T(128)S(1)} %copy-done, s32[16384]{0:T(1024)S(1)} %fusion.22), kind=kCustom, calls=%fused_computation | custom fusion | bytes 196608 | tf_op jit(solution)/shard_map/gather | solution.py:32
  105.1 0.0 copy-start.2
  105.1 0.0 copy-start.4
  105.1 97.2 %gather_fusion.1 = f32[16384]{0:T(1024)S(1)} fusion(f32[128]{0:T(128)S(1)} %copy-done, s32[16384]{0:T(1024)S(1)} %fusion.24), kind=kCustom, calls=%fused_computation.1 | custom fusion | bytes 196608 | tf_op jit(solution)/shard_map/gather | solution.py:35
  202.4 0.2 select_reduce_fusion
  202.6 0.2 select_multiply_fusion.2
  202.8 0.6 fusion.26
  203.4 0.0 copy-start.1
  203.4 0.7 fusion.16
  204.2 0.0 copy-start.3
  204.2 0.2 copy.30
  204.4 0.2 fusion.18
  204.6 0.6 fusion.39
  205.2 0.6 fusion.38
  205.8 0.6 fusion.37
  206.4 0.6 fusion.36
  207.1 0.6 fusion.35
  207.7 0.6 fusion.34
  208.3 0.6 fusion.33
  208.9 0.6 fusion.32
  209.5 7.2 %all-to-all-start = ((bf16[8,32,1,512]{3,1,2,0:T(8,128)(2,1)}), bf16[8,32,1,512]{3,1,2,0:T(8,128)(2,1)S(1)}, u32[]{:S(2)}, u32[]{:S(2)}) async-start(bf16[8,32,1,512]{3,1,2,0:T(8,128)(2,1)} %fusion.32), calls=%async_computation | async-start | bytes 524288 | tf_op jit(solution)/shard_map/all_to_all | solution.py:92
  216.8 0.0 all-reduce.6.cloned.1.call-start
  216.9 8.8 %all-to-all-done = bf16[8,32,1,512]{3,1,2,0:T(8,128)(2,1)S(1)} async-done(((bf16[8,32,1,512]{3,1,2,0:T(8,128)(2,1)}), bf16[8,32,1,512]{3,1,2,0:T(8,128)(2,1)S(1)}, u32[]{:S(2)}, u32[]{:S(2)}) %all-to-all-start) | async-done | bytes 262176 | tf_op jit(solution)/shard_map/all_to_all | solution.py:92
  225.7 0.1 copy.42
  225.9 1.3 collective-permute-start
  227.2 0.7 fusion.56
  235.4 0.6 gather_fusion.2
  236.0 0.2 copy.32
  236.2 284.2 %gather_fusion.3 = bf16[81920,4]{1,0:T(8,128)(2,1)} fusion(bf16[4,768]{0,1:T(8,128)(2,1)S(1)} %copy.32, s32[81920]{0:T(1024)S(1)} %broadcast_clamp_fusion), kind=kCustom, calls=%fused_computation.3 | custom fusion | bytes 1638400 | tf_op jit(solution)/shard_map/gather | solution.py:59
  520.3 19.5 %copy.33 = bf16[640,128,4]{0,1,2:T(8,128)(2,1)S(1)} copy(bf16[640,128,4]{2,1,0:T(8,128)(2,1)} %bitcast.125) | data formatting | bytes 1310720 | tf_op jit(solution)/shard_map/gather | solution.py:59
  539.8 0.0 collective-permute-done
  539.9 0.1 pad_maximum_fusion.1
  540.0 0.3 fusion.7
  540.3 0.3 fusion.6
  540.7 0.3 fusion.5
  541.0 0.4 fusion.4
  541.4 0.4 fusion.3
  541.7 0.3 fusion.2
  542.1 0.3 fusion.1
  542.4 0.3 fusion
  542.8 0.2 broadcast_multiply_fusion
  543.0 2.0 copy.34
  545.0 0.0 all-reduce.6.cloned.1.call-update
  545.0 0.6 copy-done.6
  545.6 0.6 dynamic-slice
  546.9 49.9 %all-reduce.6.cloned.1.call-done = f32[128,4,1024]{2,1,0:T(4,128)} async-done(((f32[128,4,1024]{2,1,0:T(4,128)}), f32[128,4,1024]{2,1,0:T(4,128)}) %all-reduce.6.cloned.1.call-update) | async-done | bytes 2097168
  596.8 1.9 constant_dynamic-slice_fusion.4
  (21 shorter events, 0.2 us)
Async XLA Ops:
  6.5 1.3 copy-start
  105.1 97.2 %copy-start.2 = (s32[1,256,1]{1,2,0:T(1,128)S(1)}, s32[1,256,1]{1,2,0:T(1,128)}, u32[]{:S(2)}) copy-start(s32[1,256,1]{1,2,0:T(1,128)} %param.9) | copy-start | bytes 3076
  105.1 97.2 %copy-start.4 = (s32[1,256,1]{1,2,0:T(1,128)S(1)}, s32[1,256,1]{1,2,0:T(1,128)}, u32[]{:S(2)}) copy-start(s32[1,256,1]{1,2,0:T(1,128)} %param.10) | copy-start | bytes 3076
  203.4 13.4 %copy-start.1 = (s32[81920]{0:T(1024)S(1)}, s32[81920]{0:T(1024)}, u32[]{:S(2)}) copy-start(s32[81920]{0:T(1024)} %constant.48) | copy-start | bytes 983044
  204.2 12.7 %copy-start.5 = (s32[4]{0:T(128)S(1)}, s32[4]{0:T(128)}, u32[]{:S(2)}) copy-start(s32[4]{0:T(128)} %param.12) | copy-start | bytes 52
  204.2 23.0 %copy-start.3 = (s32[4]{0:T(128)S(1)}, s32[4]{0:T(128)}, u32[]{:S(2)}) copy-start(s32[4]{0:T(128)} %param.13) | copy-start | bytes 52
  209.5 16.2 %all-to-all-start = ((bf16[8,32,1,512]{3,1,2,0:T(8,128)(2,1)}), bf16[8,32,1,512]{3,1,2,0:T(8,128)(2,1)S(1)}, u32[]{:S(2)}, u32[]{:S(2)}) async-start(bf16[8,32,1,512]{3,1,2,0:T(8,128)(2,1)} %fusion.32), calls=%async_computation | async-start | bytes 524288 | tf_op jit(solution)/shard_map/all_to_all | solution.py:92
  216.8 380.0 %all-reduce.6.cloned.1.call-start = ((), (), s32[]{:S(2)}) async-start(), calls=%async_computation.1 | async-start | bytes 4194304
  225.9 314.0 %collective-permute-start = (bf16[256,512]{1,0:T(8,128)(2,1)S(1)}, bf16[256,512]{1,0:T(8,128)(2,1)S(1)}, u32[]{:S(2)}, u32[]{:S(2)}) collective-permute-start(bf16[256,512]{1,0:T(8,128)(2,1)S(1)} %bitcast.129), channel_id=1, source_target_pairs={{1,0},{2,1},{3,2},{4,3},{5,4},{6,5},{7,6},{9,8},{10,9},{11,10},{12... | collective-permute-start | bytes 786440 | tf_op jit(solution)/shard_map/ppermute | solution.py:15
  545.0 0.7 copy-start.6
Sparse Core Ops, SparseCore 0:
  545.1 51.5 all-reduce.5
